TPU v7x, 256 devices: a whole 4x4x8 slice. The times are simulated.
256 devices in a mesh: srv: 2 (over core), smp: 128 (over y, z, x).
Axes of the slice: x: 4, y: 4, z: 8, core: 2. Of those that a mesh axis runs over, the one named last changes fastest.
Arguments:
- genotype_sites: float32 [2, 1024, 32768], P('srv', None, 'smp'), may hold values from -6 to 8, as said below
- covariate_sites: float32 [2, 10, 32768], P('srv', None, 'smp'), may hold values from -8 to 10
- sample_ids: int32 [32768], P('smp'), may hold values from -1 to 16383, as said below
- mask_cov_first: float32 [2, 10, 16384], P('srv', None, 'smp'), may hold values from -6 to 6
- mask_geno: float32 [2, 1024, 16384], P('srv', None, 'smp'), may hold values from -6 to 6
- prod_first: float32 [2, 10, 1024], P('srv'), as said below
- mask_cov_second: float32 [2, 10, 16384], P('srv', None, 'smp'), may hold values from -6 to 6
- mask_weight: float32 [2, 10, 1024], P('srv'), may hold values from -6 to 6
- prod_second: float32 [2, 1024, 16384], P('srv', None, 'smp'), as said below
- coef: float32 [10, 10], replicated
- phenotypes: float32 [16384, 32], P('smp'), may hold values from -6 to 6
Outputs:
- residual_share: float32 [2, 1024, 16384], P('srv', 'smp')
- score_share: float32 [2, 1024, 32], P('srv', 'smp')
Inputs may be any that keep to these rules, and one draw needn't show every extreme that they name: `sample_ids`: every individual 0 to 16383 is named exactly once, all other entries are -1. Individual i belongs to sample block i // 128. Of the 256 entries of one device at most 2 belong to one sample block, and every block has a device with exactly 2 of them. `genotype_sites`: the two servers' shares add up to genotypes 0, 1 or 2. `prod_first`: the two shares add up to the product of the summed covariate mask and the summed genotype mask over all individuals. `prod_second`: the two shares add up to the summed coefficient mask transposed times the summed covariate mask.
All inputs are finite; a program needn't handle non-finite values.
Results may differ from a plain program's by a relative error of at most 0.0001.
Values sent between devices are 32-bit elements; how exact they have to be, the bound alone decides.
No kernel may reach another device: no remote copies, remote signals or barrier semaphores. Data moves between devices by JAX's collectives and lax.ppermute only.
A program may use at most 64 MiB of HBM per device.

v0:
```python
import math
import jax
import jax.numpy as jnp
from jax import lax
from jax.sharding import PartitionSpec as P

ROWS = 128
precise = lax.Precision.HIGHEST


def from_partner(value, axis, apart):
    mask = 2**apart
    pairs = [(source, source ^ mask) for source in range(lax.axis_size(axis))]
    return lax.ppermute(value, axis, pairs)


def contract_last(left, right):
    return lax.dot_general(
        left, right, (((1,), (1,)), ((), ())), precision=precise, preferred_element_type=jnp.float32
    )


def contract_first(left, right):
    return lax.dot_general(
        left, right, (((0,), (0,)), ((), ())), precision=precise, preferred_element_type=jnp.float32
    )


def pack_columns(site_geno, site_cov, sample_ids, block_count):
    capacity = sample_ids.shape[0]
    slot_width = capacity // block_count
    is_live = sample_ids >= 0
    owner_block = jnp.where(is_live, sample_ids // ROWS, 0)
    membership = (
        (owner_block[:, None] == jnp.arange(block_count, dtype=jnp.int32)[None, :])
        & is_live[:, None]
    ).astype(jnp.int32)
    earlier_count = jnp.cumsum(membership, axis=0) - membership
    rank_within = jnp.sum(earlier_count * membership, axis=1)
    slot_index = jnp.where(is_live, owner_block * slot_width + rank_within, capacity)
    source_column = (
        jnp.zeros((capacity,), jnp.int32)
        .at[slot_index]
        .set(jnp.arange(capacity, dtype=jnp.int32), mode="drop")
    )
    slot_used = jnp.zeros((capacity,), jnp.float32).at[slot_index].set(1.0, mode="drop")
    local_row = jnp.where(is_live, sample_ids % ROWS, -1).astype(jnp.float32)
    placed_row = jnp.where(slot_used > 0, local_row[source_column], -1.0)
    packed_geno = jnp.take(site_geno, source_column, axis=1) * slot_used[None, :]
    packed_cov = jnp.take(site_cov, source_column, axis=1) * slot_used[None, :]
    return (packed_geno, packed_cov, placed_row[None, :])


def local(
    genotype_sites,
    covariate_sites,
    sample_ids,
    mask_cov_first,
    mask_geno,
    prod_first,
    mask_cov_second,
    mask_weight,
    prod_second,
    coef,
    phenotypes,
):
    block_count = lax.axis_size("smp")
    leader = (lax.axis_index("srv") == 0).astype(jnp.float32)
    packed_geno, packed_cov, placed_row = pack_columns(
        genotype_sites[0], covariate_sites[0], sample_ids, block_count
    )
    recv_geno, recv_cov, recv_row = (
        lax.all_to_all(packed_geno, "smp", split_axis=1, concat_axis=1, tiled=True),
        lax.all_to_all(packed_cov, "smp", split_axis=1, concat_axis=1, tiled=True),
        lax.all_to_all(placed_row, "smp", split_axis=1, concat_axis=1, tiled=True),
    )
    target = jnp.where(recv_row[0] >= 0, recv_row[0], float(ROWS)).astype(jnp.int32)
    block_geno = (
        jnp.zeros((recv_geno.shape[0], ROWS), jnp.float32).at[:, target].set(recv_geno, mode="drop")
    )
    block_cov = (
        jnp.zeros((recv_cov.shape[0], ROWS), jnp.float32).at[:, target].set(recv_cov, mode="drop")
    )
    masked_cov = block_cov - mask_cov_first[0]
    masked_geno = block_geno - mask_geno[0]
    masked_second = block_cov - mask_cov_second[0]
    peer_cov, peer_geno = from_partner((masked_cov, masked_geno), "srv", 0)
    open_cov = masked_cov + peer_cov
    open_geno = masked_geno + peer_geno
    partial_value = (
        contract_last(open_cov, mask_geno[0])
        + contract_last(mask_cov_first[0], open_geno)
        + leader * contract_last(open_cov, open_geno)
    )
    gram_share = prod_first[0] + lax.psum(partial_value, "smp")
    weight_share = jnp.dot(coef, gram_share, precision=precise, preferred_element_type=jnp.float32)
    masked_weight = weight_share - mask_weight[0]
    peer_second, peer_weight = from_partner((masked_second, masked_weight), "srv", 0)
    open_second = masked_second + peer_second
    open_weight = masked_weight + peer_weight
    fitted = (
        prod_second[0]
        + contract_first(mask_weight[0], open_second)
        + contract_first(open_weight, mask_cov_second[0])
        + leader * contract_first(open_weight, open_second)
    )
    residual = block_geno - fitted
    columns = lax.all_to_all(residual, "smp", split_axis=0, concat_axis=1, tiled=True)
    scale = 1.0 / math.sqrt(ROWS * block_count)
    scores = jnp.dot(
        columns,
        lax.all_gather(phenotypes, "smp", axis=0, tiled=True),
        precision=precise,
        preferred_element_type=jnp.float32,
    )
    return (columns[None], (scores * scale)[None])


def solution(mesh):
    return jax.shard_map(
        local,
        mesh=mesh,
        in_specs=(
            P("srv", None, "smp"),
            P("srv", None, "smp"),
            P("smp"),
            P("srv", None, "smp"),
            P("srv", None, "smp"),
            P("srv", None, None),
            P("srv", None, "smp"),
            P("srv", None, None),
            P("srv", None, "smp"),
            P(),
            P("smp", None),
        ),
        out_specs=(P("srv", "smp", None), P("srv", "smp", None)),
        check_vma=False,
    )
```

profile of v0, /device:TPU:32, one launch (start us, length us, event | category | flops | bytes accessed | tf_op | source)
XLA Modules:
  0.0 829.3 jit_solution(5428320511166354375)
XLA Ops:
  7.2 0.8 fusion.38
  8.9 0.7 compare_select_fusion.3
  9.6 1.4 scatter_custom_fusion.1
  11.0 1.4 scatter_custom_fusion
  12.4 1.9 gather_fusion
  14.4 0.8 all_to_all.32
  15.1 15.0 %all-to-all-start = ((f32[1,128,2]{2,0,1:T(1,128)}), f32[1,128,2]{2,0,1:T(1,128)S(1)}, u32[]{:S(2)}, u32[]{:S(2)}) async-start(f32[1,128,2]{2,0,1:T(1,128)} %bitcast.5), calls=%async_computation | async-start | bytes 131072 | tf_op jit(solution)/shard_map/all_to_all | solution.py:75
  30.7 1.1 gather_fusion.1
  31.7 0.6 gather.17
  32.5 1.6 select_multiply_fusion
  34.1 7.2 all-to-all-done
  41.3 6.6 all-to-all-start.1
  48.0 0.7 all-gather.2.cloned.1.call-update
  49.4 0.8 reduce.3
  50.4 27.2 %all-to-all-done.1 = f32[1024,128,2]{0,2,1:T(2,128)S(1)} async-done(((f32[1024,128,2]{0,2,1:T(2,128)}), f32[1024,128,2]{0,2,1:T(2,128)S(1)}, u32[]{:S(2)}, u32[]{:S(2)}) %all-to-all-start.1) | async-done | bytes 1048608 | tf_op jit(solution)/shard_map/all_to_all | solution.py:73
  77.6 0.7 reshape.136
  78.3 1.6 scatter_custom_fusion.2
  80.4 0.7 gather_fusion.2
  81.2 1.0 select_multiply_fusion.1
  82.2 7.2 all-to-all-start.2
  89.6 12.0 %all-to-all-done.2 = f32[10,128,2]{0,2,1:T(2,128)S(1)} async-done(((f32[10,128,2]{0,2,1:T(2,128)}), f32[10,128,2]{0,2,1:T(2,128)S(1)}, u32[]{:S(2)}, u32[]{:S(2)}) %all-to-all-start.2) | async-done | bytes 10272 | tf_op jit(solution)/shard_map/all_to_all | solution.py:74
  101.6 1.2 scatter_custom_fusion.3
  103.4 0.8 collective-permute-done.1
  104.6 0.6 fusion.5
  105.1 673.8 %psum.7 = f32[10,1024]{1,0:T(8,128)S(1)} all-reduce(f32[10,1024]{1,0:T(8,128)S(1)} %fusion.5), channel_id=1, replica_groups=mesh['srv'=2,'smp'=128] {'smp'}, use_global_device_ids=true, to_apply=%region_7.8 | all-reduce | flops 10240 | bytes 81920 | tf_op jit(solution)/shard_map/psum | solution.py:95
  779.4 0.6 collective-permute-start
  780.5 0.6 fusion.24
  781.0 0.6 convolution_multiply_fusion
  781.6 0.7 fusion.3
  782.5 35.2 %all_to_all.46 = f32[128,8,128]{2,1,0:T(8,128)S(1)} all-to-all(f32[128,8,128]{2,1,0:T(8,128)S(1)} %bitcast.87), channel_id=1, replica_groups=mesh['srv'=2,'smp'=128] {'smp'}, dimensions={0} | all-to-all | bytes 1048576 | tf_op jit(solution)/shard_map/all_to_all | solution.py:108
  817.7 4.0 fusion.6
  821.7 0.8 copy.61
  (59 shorter events, 5.2 us)
Async XLA Ops:
  7.2 771.7 %copy-start = (f32[10,10]{1,0:T(8,128)S(1)}, f32[10,10]{1,0:T(8,128)}, u32[]{:S(2)}) copy-start(f32[10,10]{1,0:T(8,128)} %param.20) | copy-start | bytes 1204
  7.2 23.1 %copy-start.2 = (f32[1,1024,256]{2,1,0:T(8,128)S(1)}, f32[1,1024,256]{2,1,0:T(8,128)}, u32[]{:S(2)}) copy-start(f32[1,1024,256]{2,1,0:T(8,128)} %param.11) | copy-start | bytes 3145732
  15.1 26.1 %all-to-all-start = ((f32[1,128,2]{2,0,1:T(1,128)}), f32[1,128,2]{2,0,1:T(1,128)S(1)}, u32[]{:S(2)}, u32[]{:S(2)}) async-start(f32[1,128,2]{2,0,1:T(1,128)} %bitcast.5), calls=%async_computation | async-start | bytes 131072 | tf_op jit(solution)/shard_map/all_to_all | solution.py:75
  32.5 16.2 %copy-start.1 = (f32[1,1024,128]{2,1,0:T(8,128)S(1)}, f32[1,1024,128]{2,1,0:T(8,128)}, u32[]{:S(2)}) copy-start(f32[1,1024,128]{2,1,0:T(8,128)} %param.15) | copy-start | bytes 1572868
  41.3 36.3 %all-to-all-start.1 = ((f32[1024,128,2]{0,2,1:T(2,128)}), f32[1024,128,2]{0,2,1:T(2,128)S(1)}, u32[]{:S(2)}, u32[]{:S(2)}) async-start(f32[1024,128,2]{0,2,1:T(2,128)} %select_multiply_fusion), calls=%async_computation.1 | async-start | bytes 2097152 | tf_op jit(solution)/shard_map/all_to_all | solution.py:73
  47.9 769.8 %all-gather.2.cloned.1.call-start = ((), (), s32[]{:S(2)}) async-start(), calls=%async_computation.4 | async-start | bytes 2113536 | tf_op jit(solution)/shard_map/all_gather | solution.py:112
  78.3 2.0 copy-start.6
  78.3 11.0 %copy-start.7 = (f32[1,10,128]{2,0,1:T(1,128)S(1)}, f32[1,10,128]{2,0,1:T(1,128)}, u32[]{:S(2)}) copy-start(f32[1,10,128]{2,0,1:T(1,128)} %param.14) | copy-start | bytes 15364
  78.3 11.2 %copy-start.8 = (f32[1,10,128]{2,0,1:T(1,128)S(1)}, f32[1,10,128]{2,0,1:T(1,128)}, u32[]{:S(2)}) copy-start(f32[1,10,128]{2,0,1:T(1,128)} %param.17) | copy-start | bytes 15364
  80.0 22.9 %collective-permute-start.2 = (f32[1024,128]{0,1:T(8,128)S(1)}, f32[1024,128]{0,1:T(8,128)S(1)}, u32[]{:S(2)}, u32[]{:S(2)}) collective-permute-start(f32[1024,128]{0,1:T(8,128)S(1)} %bitcast_subtract_fusion), channel_id=1, source_target_pairs={{0,128},{128,0},{1,129},{129,1},{2,130},{130,2},{3,131},{131,3},{4... | collective-permute-start | bytes 1572872 | tf_op jit(solution)/shard_map/ppermute | solution.py:14
  82.2 696.8 %copy-start.4 = (f32[1,10,1024]{2,0,1:T(1,128)S(1)}, f32[1,10,1024]{2,0,1:T(1,128)}, u32[]{:S(2)}) copy-start(f32[1,10,1024]{2,0,1:T(1,128)} %param.18) | copy-start | bytes 122884
  82.2 696.8 %copy-start.5 = (f32[1,10,1024]{2,0,1:T(1,128)S(1)}, f32[1,10,1024]{2,0,1:T(1,128)}, u32[]{:S(2)}) copy-start(f32[1,10,1024]{2,0,1:T(1,128)} %param.16) | copy-start | bytes 122884
  82.2 19.5 %all-to-all-start.2 = ((f32[10,128,2]{0,2,1:T(2,128)}), f32[10,128,2]{0,2,1:T(2,128)S(1)}, u32[]{:S(2)}, u32[]{:S(2)}) async-start(f32[10,128,2]{0,2,1:T(2,128)} %select_multiply_fusion.1), calls=%async_computation.2 | async-start | bytes 262144 | tf_op jit(solution)/shard_map/all_to_all | solution.py:74
  89.4 689.9 %copy-start.3 = (f32[1,1024,128]{2,1,0:T(8,128)S(1)}, f32[1,1024,128]{2,1,0:T(8,128)}, u32[]{:S(2)}) copy-start(f32[1,1024,128]{2,1,0:T(8,128)} %param.19) | copy-start | bytes 1572868
  102.8 1.3 collective-permute-start.1
  779.1 1.3 collective-permute-start.3
  779.4 1.6 collective-permute-start
Sparse Core Ops, SparseCore 0:
  52.2 108.3 all-gather.1
where the time goes:
time: 830 us; the launch traced here: 829 us
  blocking collectives  709 us (85%)
  waiting for transfers between devices  48.4 us (6%)
  starting transfers between devices  29.9 us (4%)
  local copies, waits for them, and re-layouts  14.7 us (2%)
  between operations  14.4 us (2%)
    psum x1, blocking collectives, local(): gram_share = prod_first[0] + lax.psum(partial_value, 'smp')  674 us
    all_to_all x1, blocking collectives, local(): lax.all_to_all(residual, 'smp', split_axis=0, concat_axis=1, tiled=True)  35.2 us
    all_to_all x1, waiting for transfers between devices, local(): lax.all_to_all(packed_geno, 'smp', split_axis=1, concat_axis=1, tiled=True)  27.2 us
  transfers between devices with their start and end apart: 8, of which 5 were waited for; matrix products, arithmetic and copies ran while one was open for 2% of the time, Pallas kernels for 0%

commit v1 on v0

--- a/solution.py
+++ b/solution.py
@@ -92,7 +92,7 @@
         + contract_last(mask_cov_first[0], open_geno)
         + leader * contract_last(open_cov, open_geno)
     )
-    gram_share = prod_first[0] + lax.psum(partial_value, "smp")
+    gram_share = prod_first[0] + jnp.sum(lax.all_gather(partial_value, "smp"), axis=0)
     weight_share = jnp.dot(coef, gram_share, precision=precise, preferred_element_type=jnp.float32)
     masked_weight = weight_share - mask_weight[0]
     peer_second, peer_weight = from_partner((masked_second, masked_weight), "srv", 0)

time: 830 us -> 344 us (0.41)
  blocking collectives: 709 us -> 29 us
  waiting for transfers between devices: 48.4 us -> 237 us
    psum x1 -> x0, blocking collectives: 674 us -> none  [local(): gram_share = prod_first[0] + lax.psum(partial_value, 'smp')]
    all_gather x0 -> x1, waiting for transfers between devices: none -> 117 us  [local(): lax.all_gather(partial_value, 'smp')]
    all_gather x1, waiting for transfers between devices: 0.01 us -> 71.1 us  [local(): lax.all_gather(phenotypes, 'smp', axis=0, tiled=True)]
  transfers between devices with their start and end apart: 8 -> 9, of which waited for: 5 -> 7; matrix products, arithmetic and copies ran while one was open for 2% -> 5% of each run, Pallas kernels for 0% -> 0%
where the time goes in v1:
time: 344 us; the launch traced here: 343 us
  waiting for transfers between devices  237 us (69%)
  starting transfers between devices  29.8 us (9%)
  blocking collectives  29 us (8%)
  local copies, waits for them, and re-layouts  14.8 us (4%)
  between operations  14.5 us (4%)
  other arithmetic  9.44 us (3%)
  matrix products  7.95 us (2%)
    all_gather x1, waiting for transfers between devices, local(): lax.all_gather(partial_value, 'smp')  117 us
    all_gather x1, waiting for transfers between devices, local(): lax.all_gather(phenotypes, 'smp', axis=0, tiled=True)  71.1 us
    all_to_all x1, blocking collectives, local(): lax.all_to_all(residual, 'smp', split_axis=0, concat_axis=1, tiled=True)  29 us
    all_to_all x1, waiting for transfers between devices, local(): lax.all_to_all(packed_geno, 'smp', split_axis=1, concat_axis=1, tiled=True)  27.9 us
    all_to_all x1, starting transfers between devices, local(): lax.all_to_all(placed_row, 'smp', split_axis=1, concat_axis=1, tiled=True)  15 us
    all_to_all x1, waiting for transfers between devices, local(): lax.all_to_all(packed_cov, 'smp', split_axis=1, concat_axis=1, tiled=True)  12 us
    all_to_all x1, waiting for transfers between devices, local(): lax.all_to_all(placed_row, 'smp', split_axis=1, concat_axis=1, tiled=True)  7.18 us
    all_to_all x1, starting transfers between devices, local(): lax.all_to_all(packed_cov, 'smp', split_axis=1, concat_axis=1, tiled=True)  7.07 us
  transfers between devices with their start and end apart: 9, of which 7 were waited for; matrix products, arithmetic and copies ran while one was open for 5% of the time, Pallas kernels for 0%

profile of v1, /device:TPU:32, one launch (start us, length us, event | category | flops | bytes accessed | tf_op | source)
XLA Modules:
  0.0 342.7 jit_solution(9110555417887391857)
XLA Ops:
  7.2 0.8 fusion.39
  8.9 0.7 compare_select_fusion.3
  9.6 1.4 scatter_custom_fusion.1
  11.0 1.4 scatter_custom_fusion
  12.4 1.9 gather_fusion
  14.4 0.8 all_to_all.32
  15.1 15.0 %all-to-all-start = ((f32[1,128,2]{2,0,1:T(1,128)}), f32[1,128,2]{2,0,1:T(1,128)S(1)}, u32[]{:S(2)}, u32[]{:S(2)}) async-start(f32[1,128,2]{2,0,1:T(1,128)} %bitcast.5), calls=%async_computation | async-start | bytes 131072 | tf_op jit(solution)/shard_map/all_to_all | solution.py:75
  30.7 1.1 gather_fusion.1
  31.7 0.6 gather.17
  32.5 1.6 select_multiply_fusion
  34.1 7.2 %all-to-all-done = f32[1,128,2]{2,0,1:T(1,128)S(1)} async-done(((f32[1,128,2]{2,0,1:T(1,128)}), f32[1,128,2]{2,0,1:T(1,128)S(1)}, u32[]{:S(2)}, u32[]{:S(2)}) %all-to-all-start) | async-done | bytes 1056 | tf_op jit(solution)/shard_map/all_to_all | solution.py:75
  41.3 6.6 %all-to-all-start.1 = ((f32[1024,128,2]{0,2,1:T(2,128)}), f32[1024,128,2]{0,2,1:T(2,128)S(1)}, u32[]{:S(2)}, u32[]{:S(2)}) async-start(f32[1024,128,2]{0,2,1:T(2,128)} %select_multiply_fusion), calls=%async_computation.1 | async-start | bytes 2097152 | tf_op jit(solution)/shard_map/all_to_all | solution.py:73
  48.7 0.8 reduce.4
  49.6 27.9 %all-to-all-done.1 = f32[1024,128,2]{0,2,1:T(2,128)S(1)} async-done(((f32[1024,128,2]{0,2,1:T(2,128)}), f32[1024,128,2]{0,2,1:T(2,128)S(1)}, u32[]{:S(2)}, u32[]{:S(2)}) %all-to-all-start.1) | async-done | bytes 1048608 | tf_op jit(solution)/shard_map/all_to_all | solution.py:73
  77.5 0.7 reshape.136
  78.2 1.6 scatter_custom_fusion.2
  80.3 0.7 gather_fusion.2
  81.1 1.0 select_multiply_fusion.1
  82.1 7.1 %all-to-all-start.2 = ((f32[10,128,2]{0,2,1:T(2,128)}), f32[10,128,2]{0,2,1:T(2,128)S(1)}, u32[]{:S(2)}, u32[]{:S(2)}) async-start(f32[10,128,2]{0,2,1:T(2,128)} %select_multiply_fusion.1), calls=%async_computation.2 | async-start | bytes 262144 | tf_op jit(solution)/shard_map/all_to_all | solution.py:74
  89.4 12.0 %all-to-all-done.2 = f32[10,128,2]{0,2,1:T(2,128)S(1)} async-done(((f32[10,128,2]{0,2,1:T(2,128)}), f32[10,128,2]{0,2,1:T(2,128)S(1)}, u32[]{:S(2)}, u32[]{:S(2)}) %all-to-all-start.2) | async-done | bytes 10272 | tf_op jit(solution)/shard_map/all_to_all | solution.py:74
  101.4 1.2 scatter_custom_fusion.3
  103.2 0.8 collective-permute-done.1
  104.4 1.2 fusion.6
  105.6 0.7 all-gather.5.cloned.1.call-update
  106.4 117.2 %all-gather.7.cloned.1.call-done = f32[128,10,1024]{2,1,0:T(8,128)} async-done(((f32[1,10,1024]{2,1,0:T(8,128)}), f32[128,10,1024]{2,1,0:T(8,128)}) %all-gather.7.cloned.1.call-update) | async-done | bytes 5242896 | tf_op jit(solution)/shard_map/all_gather | solution.py:95
  223.6 3.9 %reduce_sum.19 = f32[10,1024]{1,0:T(8,128)S(1)} reduce(f32[128,10,1024]{2,1,0:T(8,128)} %all-gather.7.cloned.1.call-done, f32[]{:T(128)} %constant.45.clone.1), dimensions={0}, to_apply=%region_7.8 | reduce | flops 1300480 | bytes 5283844 | tf_op jit(solution)/shard_map/reduce_sum | solution.py:95
  228.0 0.6 collective-permute-start
  230.2 0.7 fusion.3
  231.1 29.0 %all_to_all.46 = f32[128,8,128]{2,1,0:T(8,128)S(1)} all-to-all(f32[128,8,128]{2,1,0:T(8,128)S(1)} %bitcast.89), channel_id=1, replica_groups=mesh['srv'=2,'smp'=128] {'smp'}, dimensions={0} | all-to-all | bytes 1048576 | tf_op jit(solution)/shard_map/all_to_all | solution.py:108
  260.0 71.1 %all-gather.5.cloned.1.call-done = f32[16384,32]{0,1:T(8,128)} async-done(((f32[128,32]{0,1:T(8,128)}), f32[16384,32]{0,1:T(8,128)}) %all-gather.5.cloned.1.call-update) | async-done | bytes 2097168 | tf_op jit(solution)/shard_map/all_gather | solution.py:112
  331.1 4.0 %fusion.7 = f32[1,8,32]{2,1,0:T(8,128)} fusion(f32[16384,32]{0,1:T(8,128)} %all-gather.5.cloned.1.call-done, f32[128,8,128]{2,1,0:T(8,128)S(1)} %all_to_all.46), kind=kOutput, calls=%fused_computation.21 | convolution fusion | flops 50331904 | bytes 2622464 | tf_op jit(solution)/shard_map/dot_general | solution.py:110
  335.1 0.8 copy.61
  (62 shorter events, 6.4 us)
Async XLA Ops:
  7.2 220.3 %copy-start = (f32[10,10]{1,0:T(8,128)S(1)}, f32[10,10]{1,0:T(8,128)}, u32[]{:S(2)}) copy-start(f32[10,10]{1,0:T(8,128)} %param.20) | copy-start | bytes 1204
  7.2 23.1 %copy-start.2 = (f32[1,1024,256]{2,1,0:T(8,128)S(1)}, f32[1,1024,256]{2,1,0:T(8,128)}, u32[]{:S(2)}) copy-start(f32[1,1024,256]{2,1,0:T(8,128)} %param.11) | copy-start | bytes 3145732
  15.1 26.1 %all-to-all-start = ((f32[1,128,2]{2,0,1:T(1,128)}), f32[1,128,2]{2,0,1:T(1,128)S(1)}, u32[]{:S(2)}, u32[]{:S(2)}) async-start(f32[1,128,2]{2,0,1:T(1,128)} %bitcast.5), calls=%async_computation | async-start | bytes 131072 | tf_op jit(solution)/shard_map/all_to_all | solution.py:75
  32.5 15.4 %copy-start.1 = (f32[1,1024,128]{2,1,0:T(8,128)S(1)}, f32[1,1024,128]{2,1,0:T(8,128)}, u32[]{:S(2)}) copy-start(f32[1,1024,128]{2,1,0:T(8,128)} %param.15) | copy-start | bytes 1572868
  41.3 36.2 %all-to-all-start.1 = ((f32[1024,128,2]{0,2,1:T(2,128)}), f32[1024,128,2]{0,2,1:T(2,128)S(1)}, u32[]{:S(2)}, u32[]{:S(2)}) async-start(f32[1024,128,2]{0,2,1:T(2,128)} %select_multiply_fusion), calls=%async_computation.1 | async-start | bytes 2097152 | tf_op jit(solution)/shard_map/all_to_all | solution.py:73
  78.2 2.0 copy-start.6
  78.2 11.0 %copy-start.7 = (f32[1,10,128]{2,0,1:T(1,128)S(1)}, f32[1,10,128]{2,0,1:T(1,128)}, u32[]{:S(2)}) copy-start(f32[1,10,128]{2,0,1:T(1,128)} %param.14) | copy-start | bytes 15364
  78.2 11.1 %copy-start.8 = (f32[1,10,128]{2,0,1:T(1,128)S(1)}, f32[1,10,128]{2,0,1:T(1,128)}, u32[]{:S(2)}) copy-start(f32[1,10,128]{2,0,1:T(1,128)} %param.17) | copy-start | bytes 15364
  79.9 22.8 %collective-permute-start.2 = (f32[1024,128]{0,1:T(8,128)S(1)}, f32[1024,128]{0,1:T(8,128)S(1)}, u32[]{:S(2)}, u32[]{:S(2)}) collective-permute-start(f32[1024,128]{0,1:T(8,128)S(1)} %bitcast_subtract_fusion), channel_id=1, source_target_pairs={{0,128},{128,0},{1,129},{129,1},{2,130},{130,2},{3,131},{131,3},{4... | collective-permute-start | bytes 1572872 | tf_op jit(solution)/shard_map/ppermute | solution.py:14
  82.1 19.4 %all-to-all-start.2 = ((f32[10,128,2]{0,2,1:T(2,128)}), f32[10,128,2]{0,2,1:T(2,128)S(1)}, u32[]{:S(2)}, u32[]{:S(2)}) async-start(f32[10,128,2]{0,2,1:T(2,128)} %select_multiply_fusion.1), calls=%async_computation.2 | async-start | bytes 262144 | tf_op jit(solution)/shard_map/all_to_all | solution.py:74
  89.1 134.4 %all-gather.7.cloned.1.call-start = ((), (), s32[]{:S(2)}) async-start(), calls=%async_computation.5 | async-start | bytes 8454144 | tf_op jit(solution)/shard_map/all_gather | solution.py:95
  102.6 1.3 collective-permute-start.1
  105.6 225.5 %all-gather.5.cloned.1.call-start = ((), (), s32[]{:S(2)}) async-start(), calls=%async_computation.4 | async-start | bytes 2113536 | tf_op jit(solution)/shard_map/all_gather | solution.py:112
  106.4 121.1 %copy-start.4 = (f32[1,10,1024]{2,0,1:T(1,128)S(1)}, f32[1,10,1024]{2,0,1:T(1,128)}, u32[]{:S(2)}) copy-start(f32[1,10,1024]{2,0,1:T(1,128)} %param.18) | copy-start | bytes 122884
  106.4 121.1 %copy-start.5 = (f32[1,10,1024]{2,0,1:T(1,128)S(1)}, f32[1,10,1024]{2,0,1:T(1,128)}, u32[]{:S(2)}) copy-start(f32[1,10,1024]{2,0,1:T(1,128)} %param.16) | copy-start | bytes 122884
  106.4 121.4 %copy-start.3 = (f32[1,1024,128]{2,1,0:T(8,128)S(1)}, f32[1,1024,128]{2,1,0:T(8,128)}, u32[]{:S(2)}) copy-start(f32[1,1024,128]{2,1,0:T(8,128)} %param.19) | copy-start | bytes 1572868
  227.7 1.3 collective-permute-start.3
  228.0 1.6 collective-permute-start
Sparse Core Ops, SparseCore 0:
  105.7 117.7 all-gather.6
  227.0 104.0 all-gather.4
